TPU v7x, 512 devices: a whole 4x4x16 slice. The times are simulated.
512 devices in a mesh: seq: 32 (over y, z_lo, core), tok: 16 (over z_hi, x).
Axes of the slice: x: 4, y: 4, z: 16 (z_hi: 4, z_lo: 4; z = z_hi * 4 + z_lo), core: 2. Of those that a mesh axis runs over, the one named last changes fastest.
Arguments:
- entering: bfloat16 [32, 512, 3, 512], P('seq', 'tok'), may hold values from -0.9059806 to 0.9059806, as said below
- fresh: bfloat16 [512, 3, 512], P('tok'), may hold values from -0.9059806 to 0.9059806, as said below
- qkv_first: bfloat16 [32, 8192, 3, 512], P('seq', 'tok'), may hold values from -6 to 6
- qkv_second: bfloat16 [32, 8192, 3, 512], P('seq', 'tok'), may hold values from -6 to 6
- rates_first: float32 [32, 8192], P('seq', 'tok'), may hold values from 5.5242715e-05 to 0.0005524272
- rates_second: float32 [32, 8192], P('seq', 'tok'), may hold values from 5.5242715e-05 to 0.0005524272
Outputs:
- out_first: bfloat16 [32, 8192, 512], P('seq', 'tok')
- out_second: bfloat16 [32, 8192, 512], P('seq', 'tok')
- leaving: bfloat16 [32, 512, 3, 512], P('seq', 'tok')
Inputs may be any that keep to these rules, and one draw needn't show every extreme that they name: `entering`: fast weights of a scale near 512 ** -0.5. `fresh`: fast weights of a scale near 512 ** -0.5.
All inputs are finite; a program needn't handle non-finite values.
Results may differ from a plain program's by a relative error of at most 0.02.
Values may be sent and summed in bfloat16 or wider, within the bound.
No kernel may reach another device: no remote copies, remote signals or barrier semaphores. Data moves between devices by JAX's collectives and lax.ppermute only.
A program may use at most 64 MiB of HBM per device.

v0:
```python
import jax
import jax.numpy as jnp
from jax import lax
from jax.sharding import PartitionSpec as P


def passed_along(block, axis, distance):
    devices = range(lax.axis_size(axis))
    route = [(i - distance, i) for i in devices if i - distance in devices]
    return lax.ppermute(block, axis, route)


def renormed(weights, gradient):
    old_values = weights.astype(jnp.float32)
    stepped = old_values - gradient
    old_norm = jnp.sqrt(jnp.sum(old_values * old_values, axis=-1, keepdims=True))
    new_norm = jnp.sqrt(jnp.sum(stepped * stepped, axis=-1, keepdims=True) + 1e-06)
    return (stepped * (old_norm / new_norm)).astype(jnp.bfloat16)


def fast_tick(full_weights, own_rows, tick_data, token_rates):
    queries = tick_data[:, 0, :]
    key_rows = tick_data[:, 1, :]
    value_rows = tick_data[:, 2, :]
    token_count = queries.shape[0]
    contract = (((1,), (1,)), ((), ()))
    across = (((0,), (0,)), ((), ()))
    stacked = jnp.concatenate([queries, key_rows], axis=0)
    pre_gate = lax.dot_general(
        stacked, full_weights[:, 0, :], contract, preferred_element_type=jnp.float32
    )
    pre_up = lax.dot_general(
        stacked, full_weights[:, 1, :], contract, preferred_element_type=jnp.float32
    )
    hidden = (jax.nn.silu(pre_gate) * pre_up).astype(jnp.bfloat16)
    output = jnp.dot(
        hidden[:token_count], full_weights[:, 2, :], preferred_element_type=jnp.float32
    ).astype(jnp.bfloat16)
    hidden_k = hidden[token_count:]
    gate_k = pre_gate[token_count:]
    up_k = pre_up[token_count:]
    scaled = (-token_rates[:, None] * value_rows.astype(jnp.float32)).astype(jnp.bfloat16)
    d_hidden = lax.dot_general(
        scaled, full_weights[:, 2, :], contract, preferred_element_type=jnp.float32
    )
    sigmoid_gate = jax.nn.sigmoid(gate_k)
    d_gate = (d_hidden * up_k * sigmoid_gate * (1.0 + gate_k * (1.0 - sigmoid_gate))).astype(
        jnp.bfloat16
    )
    d_up = (d_hidden * jax.nn.silu(gate_k)).astype(jnp.bfloat16)
    gradient = lax.psum_scatter(
        jnp.stack(
            [
                lax.dot_general(d_gate, key_rows, across, preferred_element_type=jnp.float32),
                lax.dot_general(d_up, key_rows, across, preferred_element_type=jnp.float32),
                lax.dot_general(hidden_k, scaled, across, preferred_element_type=jnp.float32),
            ],
            axis=1,
        ).astype(jnp.bfloat16),
        "tok",
        scatter_dimension=0,
        tiled=True,
    ).astype(jnp.float32)
    new_rows = renormed(own_rows, gradient)
    return (output, new_rows, None)


def on_device(entering, fresh, qkv_first, qkv_second, rates_first, rates_second):
    own_rows = entering[0]
    row_count = own_rows.shape[0]
    full_weights = lax.all_gather(own_rows, "tok", axis=0, tiled=True)
    out_first, new_rows, new_full = fast_tick(full_weights, own_rows, qkv_first[0], rates_first[0])
    first_group = lax.axis_index("seq") == 0
    next_full = lax.all_gather(new_rows, "tok", axis=0, tiled=True)
    received = passed_along(next_full, "seq", 1)
    fresh_full = lax.all_gather(fresh, "tok", axis=0, tiled=True)
    second_full = jnp.where(first_group, fresh_full, received)
    second_rows = lax.dynamic_slice_in_dim(
        second_full, lax.axis_index("tok") * row_count, row_count, 0
    )
    out_second, leaving_rows, unused_full = fast_tick(
        second_full, second_rows, qkv_second[0], rates_second[0]
    )
    return (out_first[None], out_second[None], leaving_rows[None])


def solution(mesh):
    placed = (
        P("seq", "tok", None, None),
        P("tok", None, None),
        P("seq", "tok", None, None),
        P("seq", "tok", None, None),
        P("seq", "tok"),
        P("seq", "tok"),
    )
    return jax.shard_map(
        on_device,
        mesh=mesh,
        in_specs=placed,
        out_specs=(P("seq", "tok", None), P("seq", "tok", None), P("seq", "tok", None, None)),
        check_vma=False,
    )
```

profile of v0, /device:TPU:8, one launch (start us, length us, event | category | flops | bytes accessed | tf_op | source)
XLA Modules:
  0.0 524.1 jit_solution(5767093935825023310)
XLA Ops:
  7.2 0.0 all-gather.9.cloned.1.call-start
  7.2 0.7 all-gather.9.cloned.1.call-update
  7.9 0.0 reduce-scatter.3.cloned.1.call-start
  7.9 0.7 neg.39
  8.6 1.3 slice_bitcast_fusion.13
  9.9 92.6 %all-gather.9.cloned.1.call-done = bf16[1,512,3,512]{3,1,2,0:T(8,128)(2,1)} async-done(((bf16[1,32,3,512]{3,1,2,0:T(8,128)(2,1)}), bf16[1,512,3,512]{3,1,2,0:T(8,128)(2,1)}) %all-gather.9.cloned.1.call-update) | async-done | bytes 1572880 | tf_op jit(solution)/shard_map/all_gather | solution.py:71
  102.5 0.0 copy-start.6
  102.5 1.9 fusion.23
  104.4 0.0 copy-done.6
  104.4 0.0 copy-start.1
  104.4 1.0 multiply_convert_fusion.1
  105.4 0.0 copy-start.7
  105.4 0.4 copy-done.1
  105.8 0.5 fusion.30
  106.3 0.5 fusion.3
  106.8 0.0 copy-done.7
  106.8 0.6 fusion.2
  107.4 0.8 fusion.1
  108.2 1.3 pad_maximum_fusion
  109.5 0.0 copy-start
  109.5 0.0 copy-start.5
  109.5 0.0 reduce-scatter.3.cloned.1.call-update
  109.5 0.0 all-gather.7.cloned.1.call-start
  109.5 112.8 %reduce-scatter.3.cloned.1.call-done = bf16[32,3,512]{2,0,1:T(8,128)(2,1)} async-done(((bf16[512,3,512]{2,0,1:T(8,128)(2,1)}), bf16[32,3,512]{2,0,1:T(8,128)(2,1)}) %reduce-scatter.3.cloned.1.call-update) | async-done | bytes 98320 | tf_op jit(solution)/shard_map/reduce_scatter | solution.py:51
  222.4 0.0 copy-done
  222.4 1.0 fusion.47
  223.4 1.6 multiply_convert_fusion.7
  225.0 0.0 all-gather.7.cloned.1.call-update
  225.1 0.0 all-gather.5.cloned.1.call-start
  225.1 0.5 all-gather.5.cloned.1.call-update
  225.6 0.0 reduce-scatter.5.cloned.1.call-start
  225.7 81.8 %all-gather.7.cloned.1.call-done = bf16[512,3,512]{2,0,1:T(8,128)(2,1)} async-done(((bf16[32,3,512]{2,0,1:T(8,128)(2,1)}), bf16[512,3,512]{2,0,1:T(8,128)(2,1)}) %all-gather.7.cloned.1.call-update) | async-done | bytes 1572880 | tf_op jit(solution)/shard_map/all_gather | solution.py:74
  307.5 1.9 collective-permute-start
  309.4 0.0 copy-done.5
  309.4 2.2 slice_bitcast_fusion.6
  311.6 83.7 %all-gather.5.cloned.1.call-done = bf16[512,3,512]{2,0,1:T(8,128)(2,1)} async-done(((bf16[32,3,512]{2,0,1:T(8,128)(2,1)}), bf16[512,3,512]{2,0,1:T(8,128)(2,1)}) %all-gather.5.cloned.1.call-update) | async-done | bytes 1572880 | tf_op jit(solution)/shard_map/all_gather | solution.py:76
  395.4 0.0 copy-start.3
  395.4 0.0 copy-start.4
  395.4 0.0 collective-permute-done
  395.4 0.2 broadcast_select_fusion
  395.6 0.8 copy-done.3
  396.4 0.2 copy-done.4
  396.6 0.7 fusion.21
  397.3 0.0 copy-start.2
  397.3 1.0 multiply_convert_fusion
  398.3 0.0 copy-start.9
  398.3 0.4 copy-done.2
  398.7 0.5 fusion.26
  399.2 0.1 copy-done.9
  399.3 0.5 fusion.7
  399.8 0.5 fusion.6
  400.4 0.8 fusion.5
  401.2 1.3 pad_maximum_fusion.1
  402.5 0.0 copy-start.8
  402.5 0.0 reduce-scatter.5.cloned.1.call-update
  402.5 1.2 copy-done.8
  403.7 0.0 copy-start.10
  403.7 2.4 fusion
  406.1 0.0 copy-done.10
  406.1 1.2 fusion.4
  407.3 107.6 %reduce-scatter.5.cloned.1.call-done = bf16[32,3,512]{2,0,1:T(8,128)(2,1)} async-done(((bf16[512,3,512]{2,0,1:T(8,128)(2,1)}), bf16[32,3,512]{2,0,1:T(8,128)(2,1)}) %reduce-scatter.5.cloned.1.call-update) | async-done | bytes 98320 | tf_op jit(solution)/shard_map/reduce_scatter | solution.py:51
  514.9 1.0 fusion.46
  516.0 1.6 fusion.48
  (3 shorter events, 0.0 us)
Async XLA Ops:
  7.2 95.3 %all-gather.9.cloned.1.call-start = ((), (), s32[]{:S(2)}) async-start(), calls=%async_computation.6 | async-start | bytes 1671168 | tf_op jit(solution)/shard_map/all_gather | solution.py:71
  7.9 214.5 %reduce-scatter.3.cloned.1.call-start = ((), (), s32[]{:S(2)}) async-start(), calls=%async_computation.3 | async-start | bytes 1671168 | tf_op jit(solution)/shard_map/reduce_scatter | solution.py:51
  102.5 1.9 copy-start.6
  104.4 1.4 copy-start.1
  105.4 1.5 copy-start.7
  109.5 112.9 %copy-start = (bf16[1,32,3,512]{3,1,2,0:T(8,128)(2,1)S(1)}, bf16[1,32,3,512]{3,1,2,0:T(8,128)(2,1)}, u32[]{:S(2)}) copy-start(bf16[1,32,3,512]{3,1,2,0:T(8,128)(2,1)} %param.6) | copy-start | bytes 294916
  109.5 199.9 %copy-start.5 = (f32[1,512]{1,0:T(1,128)S(1)}, f32[1,512]{1,0:T(1,128)}, u32[]{:S(2)}) copy-start(f32[1,512]{1,0:T(1,128)} %param.11) | copy-start | bytes 6148
  109.5 198.0 %all-gather.7.cloned.1.call-start = ((), (), s32[]{:S(2)}) async-start(), calls=%async_computation.4 | async-start | bytes 1671168 | tf_op jit(solution)/shard_map/all_gather | solution.py:74
  225.1 170.3 %all-gather.5.cloned.1.call-start = ((), (), s32[]{:S(2)}) async-start(), calls=%async_computation.2 | async-start | bytes 1671168 | tf_op jit(solution)/shard_map/all_gather | solution.py:76
  225.6 289.3 %reduce-scatter.5.cloned.1.call-start = ((), (), s32[]{:S(2)}) async-start(), calls=%async_computation.5 | async-start | bytes 1671168 | tf_op jit(solution)/shard_map/reduce_scatter | solution.py:51
  307.5 87.9 %collective-permute-start = (bf16[512,3,512]{2,0,1:T(8,128)(2,1)}, bf16[512,3,512]{2,0,1:T(8,128)(2,1)S(1)}, u32[]{:S(2)}, u32[]{:S(2)}) collective-permute-start(bf16[512,3,512]{2,0,1:T(8,128)(2,1)} %all-gather.7.cloned.1.call-done), channel_id=1, source_target_pairs={{0,16},{16,32},{32,48},{48,64},{64,80},{80,96},{96,112},{112,128},... | collective-permute-start | bytes 4718600 | tf_op jit(solution)/shard_map/ppermute | solution.py:10
  395.4 1.0 copy-start.3
  395.4 1.2 copy-start.4
  397.3 1.4 copy-start.2
  398.3 1.0 copy-start.9
  402.5 1.2 copy-start.8
  403.7 2.4 copy-start.10
Sparse Core Ops, SparseCore 0:
  11.0 91.4 all-gather.8
  109.6 112.7 reduce-scatter.2
  226.0 81.4 all-gather.6
  310.3 84.9 all-gather.4
  402.6 112.2 reduce-scatter.4
where the time goes:
time: 525 us; the launch traced here: 524 us
  waiting for transfers between devices  480 us (91%)
  between operations  14 us (3%)
  matrix products  12.8 us (2%)
  other arithmetic  8.81 us (2%)
  local copies, waits for them, and re-layouts  6.63 us (1%)
    reduce_scatter x2, waiting for transfers between devices, fast_tick(): lax.psum_scatter(jnp.stack([lax.dot_general(d_gate, key_rows, across, pre...  220 us
    all_gather x1, waiting for transfers between devices, on_device(): full_weights = lax.all_gather(own_rows, 'tok', axis=0, tiled=True)  92.6 us
    all_gather x1, waiting for transfers between devices, on_device(): fresh_full = lax.all_gather(fresh, 'tok', axis=0, tiled=True)  83.7 us
    all_gather x1, waiting for transfers between devices, on_device(): next_full = lax.all_gather(new_rows, 'tok', axis=0, tiled=True)  81.8 us
  transfers between devices with their start and end apart: 6, of which 5 were waited for; matrix products, arithmetic and copies ran while one was open for 1% of the time, Pallas kernels for 0%

commit v1 on v0

v1 whole, which is shorter than its diff:
```python
import jax
import jax.numpy as jnp
from jax import lax
from jax.sharding import PartitionSpec as P

SIDE = 4


def far_groups(size):
    return [[near + SIDE * far for far in range(size // SIDE)] for near in range(SIDE)]


def near_groups(size):
    return [[near + SIDE * far for near in range(SIDE)] for far in range(size // SIDE)]


def gathered(rows, groups):
    return lax.all_gather(rows, "tok", axis=0, axis_index_groups=groups)


def exchanged(blocks, groups):
    return lax.all_to_all(blocks, "tok", 0, 0, axis_index_groups=groups, tiled=True)


def summed(blocks):
    return jnp.sum(blocks.astype(jnp.float32), axis=0)


def renormed(weights, gradient):
    old_values = weights.astype(jnp.float32)
    stepped = old_values - gradient
    old_norm = jnp.sqrt(jnp.sum(old_values * old_values, axis=-1, keepdims=True))
    new_norm = jnp.sqrt(jnp.sum(stepped * stepped, axis=-1, keepdims=True) + 1e-06)
    return (stepped * (old_norm / new_norm)).astype(jnp.bfloat16)


def widened(rows):
    size = lax.axis_size("tok")
    column = gathered(rows, far_groups(size))
    half = column.shape[2] // 2
    flat = column.reshape(column.shape[0], -1, column.shape[-1])
    middle = flat.shape[1] // 2
    first = gathered(flat[:, :middle], near_groups(size))
    second = gathered(flat[:, middle:], near_groups(size))
    return jnp.concatenate([first, second], axis=2).reshape(
        (SIDE,) + column.shape
    )


def fast_tick(own_rows, tick_data, token_rates):
    size = lax.axis_size("tok")
    full = widened(own_rows)
    width = full.shape[-1]
    gate_rows = full[:, :, 0].reshape(-1, width)
    up_rows = full[:, :, 1].reshape(-1, width)
    down_rows = full[:, :, 2].reshape(-1, width)
    queries, key_rows, value_rows = tick_data
    token_count = queries.shape[0]
    contract = (((1,), (1,)), ((), ()))
    across = (((0,), (0,)), ((), ()))
    stacked = jnp.concatenate([queries, key_rows], axis=0)
    pre_gate = lax.dot_general(stacked, gate_rows, contract, preferred_element_type=jnp.float32)
    pre_up = lax.dot_general(stacked, up_rows, contract, preferred_element_type=jnp.float32)
    hidden = (jax.nn.silu(pre_gate) * pre_up).astype(jnp.bfloat16)
    output = jnp.dot(
        hidden[:token_count], down_rows, preferred_element_type=jnp.float32
    ).astype(jnp.bfloat16)
    hidden_k = hidden[token_count:]
    gate_k = pre_gate[token_count:]
    up_k = pre_up[token_count:]
    scaled = (-token_rates[:, None] * value_rows.astype(jnp.float32)).astype(jnp.bfloat16)
    d_hidden = lax.dot_general(scaled, down_rows, contract, preferred_element_type=jnp.float32)
    sigmoid_gate = jax.nn.sigmoid(gate_k)
    d_gate = (d_hidden * up_k * sigmoid_gate * (1.0 + gate_k * (1.0 - sigmoid_gate))).astype(
        jnp.bfloat16
    )
    d_up = (d_hidden * jax.nn.silu(gate_k)).astype(jnp.bfloat16)
    block = full.shape[:2] + full.shape[3:]
    partial = jnp.stack(
        [
            lax.dot_general(left, right, across, preferred_element_type=jnp.float32)
            .astype(jnp.bfloat16)
            .reshape(block)
            for left, right in ((d_gate, key_rows), (d_up, key_rows), (hidden_k, scaled))
        ],
        axis=2,
    )
    column = summed(exchanged(partial, near_groups(size))).astype(jnp.bfloat16)
    gradient = summed(exchanged(column, far_groups(size)))
    return output, renormed(own_rows, gradient)


def on_device(entering, fresh, qkv_first, qkv_second, rates_first, rates_second):
    groups = lax.axis_size("seq")
    own_rows = jnp.swapaxes(entering[0], 0, 1)
    fresh_rows = jnp.swapaxes(fresh, 0, 1)
    first_data = tuple(qkv_first[0][:, i, :] for i in range(3))
    second_data = tuple(qkv_second[0][:, i, :] for i in range(3))
    out_first, new_rows = fast_tick(own_rows, first_data, rates_first[0])
    last_group = lax.axis_index("seq") == groups - 1
    handed = jnp.where(last_group, fresh_rows, new_rows)
    second_rows = lax.ppermute(handed, "seq", [(i, (i + 1) % groups) for i in range(groups)])
    out_second, leaving_rows = fast_tick(second_rows, second_data, rates_second[0])
    leaving = jnp.swapaxes(leaving_rows, 0, 1)
    return (out_first[None], out_second[None], leaving[None])


def solution(mesh):
    placed = (
        P("seq", "tok", None, None),
        P("tok", None, None),
        P("seq", "tok", None, None),
        P("seq", "tok", None, None),
        P("seq", "tok"),
        P("seq", "tok"),
    )
    return jax.shard_map(
        on_device,
        mesh=mesh,
        in_specs=placed,
        out_specs=(P("seq", "tok", None), P("seq", "tok", None), P("seq", "tok", None, None)),
        check_vma=False,
    )
```

time: 525 us -> 215 us (0.41)
  waiting for transfers between devices: 480 us -> 40.3 us
  blocking collectives: 0 us -> 139 us
  starting transfers between devices: 2.1 us -> 15.5 us
  between operations: 14 us -> 0.94 us
  other arithmetic: 8.81 us -> 2.39 us
    all_gather x3 -> x0, waiting for transfers between devices: 258 us -> none  [the longest x1 92.6 us: on_device(): full_weights = lax.all_gather(own_rows, 'tok', axis=0, tiled=True)]
    reduce_scatter x2 -> x0, waiting for transfers between devices: 220 us -> none  [fast_tick(): lax.psum_scatter(jnp.stack([lax.dot_general(d_gate, key_rows, across, pre...]
    all_gather x0 -> x6, blocking collectives: none -> 106 us  [gathered(): return lax.all_gather(rows, 'tok', axis=0, axis_index_groups=groups)]
    all_to_all x0 -> x2, waiting for transfers between devices: none -> 33.6 us  [exchanged(): lax.all_to_all(blocks, 'tok', 0, 0, axis_index_groups=groups, tiled=True)]
    all_to_all x0 -> x2, blocking collectives: none -> 33.6 us  [exchanged(): lax.all_to_all(blocks, 'tok', 0, 0, axis_index_groups=groups, tiled=True)]
    all_to_all x0 -> x2, starting transfers between devices: none -> 13.6 us  [exchanged(): lax.all_to_all(blocks, 'tok', 0, 0, axis_index_groups=groups, tiled=True)]
    ppermute x1, waiting for transfers between devices: 0.01 us -> 6.67 us  [on_device(): lax.ppermute(handed, 'seq', [(i, (i + 1) % groups) for i in range(groups)])]
  transfers between devices with their start and end apart: 6 -> 3, of which waited for: 5 -> 3; matrix products, arithmetic and copies ran while one was open for 1% -> 2% of each run, Pallas kernels for 0% -> 0%
where the time goes in v1:
time: 215 us; the launch traced here: 214 us
  blocking collectives  139 us (65%)
  waiting for transfers between devices  40.3 us (19%)
  starting transfers between devices  15.5 us (7%)
  matrix products  11.6 us (5%)
  local copies, waits for them, and re-layouts  4.26 us (2%)
  other arithmetic  2.39 us (1%)
    all_gather x6, blocking collectives, gathered(): return lax.all_gather(rows, 'tok', axis=0, axis_index_groups=groups)  106 us
    all_to_all x2, waiting for transfers between devices, exchanged(): lax.all_to_all(blocks, 'tok', 0, 0, axis_index_groups=groups, tiled=True)  33.6 us
    all_to_all x2, blocking collectives, exchanged(): lax.all_to_all(blocks, 'tok', 0, 0, axis_index_groups=groups, tiled=True)  33.6 us
    all_to_all x2, starting transfers between devices, exchanged(): lax.all_to_all(blocks, 'tok', 0, 0, axis_index_groups=groups, tiled=True)  13.6 us
    ppermute x1, waiting for transfers between devices, on_device(): lax.ppermute(handed, 'seq', [(i, (i + 1) % groups) for i in range(groups)])  6.67 us
  transfers between devices with their start and end apart: 3, of which 3 were waited for; matrix products, arithmetic and copies ran while one was open for 2% of the time, Pallas kernels for 0%

profile of v1, /device:TPU:8, one launch (start us, length us, event | category | flops | bytes accessed | tf_op | source)
XLA Modules:
  0.0 214.4 jit_solution(1640853351747871515)
XLA Ops:
  0.6 30.7 %all-gather = bf16[12,32,512]{2,1,0:T(8,128)(2,1)S(1)} all-gather(bf16[3,32,512]{2,1,0:T(8,128)(2,1)} %bitcast.116), channel_id=2, replica_groups={{0,4,8,12},{1,5,9,13},{2,6,10,14},{3,7,11,15},{16,20,24,28},{17,21,25,2..., dimensions={0}, use_global_device_ids=true | all-gather | bytes 491520 | tf_op jit(solution)/shard_map/all_gather | solution.py:18
  31.4 14.3 %all-gather.2 = bf16[16,48,512]{2,1,0:T(8,128)(2,1)S(1)} all-gather(bf16[4,48,512]{2,1,0:T(8,128)(2,1)S(1)} %get-tuple-element.20), channel_id=4, replica_groups={{0,1,2,3},{4,5,6,7},{8,9,10,11},{12,13,14,15},{16,17,18,19},{20,21,22,2..., dimensions={0}, use_global_device_ids=true | all-gather | bytes 983040 | tf_op jit(solution)/shard_map/all_gather | solution.py:18
  45.7 13.3 %all-gather.1 = bf16[16,48,512]{2,1,0:T(8,128)(2,1)S(1)} all-gather(bf16[4,48,512]{2,1,0:T(8,128)(2,1)S(1)} %get-tuple-element.19), channel_id=3, replica_groups={{0,1,2,3},{4,5,6,7},{8,9,10,11},{12,13,14,15},{16,17,18,19},{20,21,22,2..., dimensions={0}, use_global_device_ids=true | all-gather | bytes 983040 | tf_op jit(solution)/shard_map/all_gather | solution.py:18
  59.0 0.1 pad_maximum_fusion
  59.1 0.0 copy-start
  59.1 0.0 copy-start.4
  59.1 0.1 fusion.53
  59.3 1.2 copy-done
  60.5 0.1 slice_bitcast_fusion.3
  60.6 0.0 copy-done.4
  60.6 0.7 fusion.17
  61.4 1.0 multiply_convert_fusion.1
  62.4 0.0 copy-start.6
  62.4 0.5 convolution_convert_fusion.4
  62.9 0.4 copy-done.6
  63.3 0.5 fusion.24
  63.8 0.5 convolution_convert_fusion.5
  64.4 0.8 convolution_convert_fusion.6
  65.1 0.2 pad_maximum_fusion.1
  65.3 17.4 %all_to_all.20 = bf16[4,4,3,32,512]{4,3,1,2,0:T(8,128)(2,1)S(1)} all-to-all(bf16[4,4,3,32,512]{4,3,1,2,0:T(8,128)(2,1)S(1)} %pad_maximum_fusion.1), channel_id=1, replica_groups={{0,1,2,3},{4,5,6,7},{8,9,10,11},{12,13,14,15},{16,17,18,19},{20,21,22,2..., dimensions={0} | all-to-all | bytes 3145728 | tf_op jit(solution)/shard_map/all_to_all | solution.py:22
  82.7 0.0 copy-start.2
  82.7 0.0 copy-start.3
  82.7 0.3 reduce_sum.78
  83.0 0.0 copy-start.1
  83.0 0.8 copy.21
  83.8 0.0 copy-start.5
  83.8 6.9 %all-to-all-start.1 = ((bf16[4,3,32,512]{3,2,1,0:T(8,128)(2,1)}), bf16[4,3,32,512]{3,2,1,0:T(8,128)(2,1)S(1)}, u32[]{:S(2)}, u32[]{:S(2)}) async-start(bf16[4,3,32,512]{3,2,1,0:T(8,128)(2,1)} %copy.21), calls=%async_computation.1 | async-start | bytes 786432 | tf_op jit(solution)/shard_map/all_to_all | solution.py:22
  90.7 19.7 %all-to-all-done.1 = bf16[4,3,32,512]{3,2,1,0:T(8,128)(2,1)S(1)} async-done(((bf16[4,3,32,512]{3,2,1,0:T(8,128)(2,1)}), bf16[4,3,32,512]{3,2,1,0:T(8,128)(2,1)S(1)}, u32[]{:S(2)}, u32[]{:S(2)}) %all-to-all-start.1) | async-done | bytes 393248 | tf_op jit(solution)/shard_map/all_to_all | solution.py:22
  110.4 0.1 convert_reduce_fusion.1
  110.4 0.0 copy-done.2
  110.4 0.1 fusion.40
  110.6 0.0 copy-done.3
  110.6 0.1 fusion.42
  110.7 1.9 collective-permute-start
  112.6 0.0 copy-done.1
  112.6 0.1 slice_bitcast_fusion.1
  112.7 0.0 copy-done.5
  112.7 6.7 %collective-permute-done = bf16[3,32,512]{2,1,0:T(8,128)(2,1)S(1)} collective-permute-done((bf16[3,32,512]{2,1,0:T(8,128)(2,1)S(1)}, bf16[3,32,512]{2,1,0:T(8,128)(2,1)S(1)}, u32[]{:S(2)}, u32[]{:S(2)}) %collective-permute-start) | collective-permute-done | bytes 98336 | tf_op jit(solution)/shard_map/ppermute | solution.py:102
  119.4 19.7 %all-gather.3 = bf16[12,32,512]{2,1,0:T(8,128)(2,1)S(1)} all-gather(bf16[3,32,512]{2,1,0:T(8,128)(2,1)S(1)} %collective-permute-done), channel_id=5, replica_groups={{0,4,8,12},{1,5,9,13},{2,6,10,14},{3,7,11,15},{16,20,24,28},{17,21,25,2..., dimensions={0}, use_global_device_ids=true | all-gather | bytes 491520 | tf_op jit(solution)/shard_map/all_gather | solution.py:18
  139.1 14.5 %all-gather.5 = bf16[16,48,512]{2,1,0:T(8,128)(2,1)S(1)} all-gather(bf16[4,48,512]{2,1,0:T(8,128)(2,1)S(1)} %get-tuple-element.18), channel_id=7, replica_groups={{0,1,2,3},{4,5,6,7},{8,9,10,11},{12,13,14,15},{16,17,18,19},{20,21,22,2..., dimensions={0}, use_global_device_ids=true | all-gather | bytes 983040 | tf_op jit(solution)/shard_map/all_gather | solution.py:18
  153.6 13.3 %all-gather.4 = bf16[16,48,512]{2,1,0:T(8,128)(2,1)S(1)} all-gather(bf16[4,48,512]{2,1,0:T(8,128)(2,1)S(1)} %get-tuple-element.17), channel_id=6, replica_groups={{0,1,2,3},{4,5,6,7},{8,9,10,11},{12,13,14,15},{16,17,18,19},{20,21,22,2..., dimensions={0}, use_global_device_ids=true | all-gather | bytes 983040 | tf_op jit(solution)/shard_map/all_gather | solution.py:18
  166.9 0.1 pad_maximum_fusion.2
  167.1 0.2 fusion.52
  167.2 0.7 fusion.15
  168.0 1.0 multiply_convert_fusion
  169.0 0.0 copy-start.7
  169.0 0.5 convolution_convert_fusion
  169.5 0.5 copy-done.7
  170.0 0.5 fusion.20
  170.5 0.6 convolution_convert_fusion.1
  171.1 0.8 convolution_convert_fusion.2
  171.8 0.2 pad_maximum_fusion.3
  172.0 16.2 %all_to_all.21 = bf16[4,4,3,32,512]{4,3,1,2,0:T(8,128)(2,1)S(1)} all-to-all(bf16[4,4,3,32,512]{4,3,1,2,0:T(8,128)(2,1)S(1)} %pad_maximum_fusion.3), channel_id=1, replica_groups={{0,1,2,3},{4,5,6,7},{8,9,10,11},{12,13,14,15},{16,17,18,19},{20,21,22,2..., dimensions={0} | all-to-all | bytes 3145728 | tf_op jit(solution)/shard_map/all_to_all | solution.py:22
  188.2 0.3 reduce_sum.82
  188.5 0.0 copy-start.8
  188.5 0.8 copy.26
  189.3 6.7 %all-to-all-start.3 = ((bf16[4,3,32,512]{3,2,1,0:T(8,128)(2,1)}), bf16[4,3,32,512]{3,2,1,0:T(8,128)(2,1)S(1)}, u32[]{:S(2)}, u32[]{:S(2)}) async-start(bf16[4,3,32,512]{3,2,1,0:T(8,128)(2,1)} %copy.26), calls=%async_computation.3 | async-start | bytes 786432 | tf_op jit(solution)/shard_map/all_to_all | solution.py:22
  196.0 2.3 %fusion = bf16[1,512,512]{2,1,0:T(8,128)(2,1)} fusion(bf16[512,512]{1,0:T(8,128)(2,1)S(1)} %bitcast.99, bf16[1024,512]{1,0:T(8,128)(2,1)} %copy-done.6), kind=kOutput, calls=%fused_computation.18 | convolution fusion | flops 268697600 | bytes 1572864 | tf_op jit(solution)/shard_map/dot_general | solution.py:65
  198.3 0.0 copy-done.8
  198.3 1.2 fusion.1
  199.5 14.0 %all-to-all-done.3 = bf16[4,3,32,512]{3,2,1,0:T(8,128)(2,1)S(1)} async-done(((bf16[4,3,32,512]{3,2,1,0:T(8,128)(2,1)}), bf16[4,3,32,512]{3,2,1,0:T(8,128)(2,1)S(1)}, u32[]{:S(2)}, u32[]{:S(2)}) %all-to-all-start.3) | async-done | bytes 393248 | tf_op jit(solution)/shard_map/all_to_all | solution.py:22
  213.5 0.1 convert_reduce_fusion
  213.6 0.1 fusion.41
  213.7 0.7 fusion.43
  (6 shorter events, 0.1 us)
Async XLA Ops:
  59.1 1.4 copy-start
  59.1 1.5 copy-start.4
  62.4 1.0 copy-start.6
  82.7 27.7 %copy-start.2 = (bf16[1,32,3,512]{3,1,2,0:T(8,128)(2,1)S(1)}, bf16[1,32,3,512]{3,1,2,0:T(8,128)(2,1)}, u32[]{:S(2)}) copy-start(bf16[1,32,3,512]{3,1,2,0:T(8,128)(2,1)} %param.6) | copy-start | bytes 294916
  82.7 27.8 %copy-start.3 = (bf16[32,3,512]{2,0,1:T(8,128)(2,1)S(1)}, bf16[32,3,512]{2,0,1:T(8,128)(2,1)}, u32[]{:S(2)}) copy-start(bf16[32,3,512]{2,0,1:T(8,128)(2,1)} %param.7) | copy-start | bytes 294916
  83.0 29.6 %copy-start.1 = (bf16[1,512,3,512]{3,1,2,0:T(8,128)(2,1)S(1)}, bf16[1,512,3,512]{3,1,2,0:T(8,128)(2,1)}, u32[]{:S(2)}) copy-start(bf16[1,512,3,512]{3,1,2,0:T(8,128)(2,1)} %param.9) | copy-start | bytes 4718596
  83.8 28.9 %copy-start.5 = (f32[1,512]{1,0:T(1,128)S(1)}, f32[1,512]{1,0:T(1,128)}, u32[]{:S(2)}) copy-start(f32[1,512]{1,0:T(1,128)} %param.11) | copy-start | bytes 6148
  83.8 26.6 %all-to-all-start.1 = ((bf16[4,3,32,512]{3,2,1,0:T(8,128)(2,1)}), bf16[4,3,32,512]{3,2,1,0:T(8,128)(2,1)S(1)}, u32[]{:S(2)}, u32[]{:S(2)}) async-start(bf16[4,3,32,512]{3,2,1,0:T(8,128)(2,1)} %copy.21), calls=%async_computation.1 | async-start | bytes 786432 | tf_op jit(solution)/shard_map/all_to_all | solution.py:22
  110.7 8.7 %collective-permute-start = (bf16[3,32,512]{2,1,0:T(8,128)(2,1)S(1)}, bf16[3,32,512]{2,1,0:T(8,128)(2,1)S(1)}, u32[]{:S(2)}, u32[]{:S(2)}) collective-permute-start(bf16[3,32,512]{2,1,0:T(8,128)(2,1)S(1)} %fusion.42), channel_id=1, source_target_pairs={{0,16},{16,32},{32,48},{48,64},{64,80},{80,96},{96,112},{112,128},... | collective-permute-start | bytes 294920 | tf_op jit(solution)/shard_map/ppermute | solution.py:102
  169.0 1.0 copy-start.7
  188.5 9.8 %copy-start.8 = (bf16[1024,512]{1,0:T(8,128)(2,1)S(1)}, bf16[1024,512]{1,0:T(8,128)(2,1)}, u32[]{:S(2)}) copy-start(bf16[1024,512]{1,0:T(8,128)(2,1)} %copy-done.7) | copy-start | bytes 3145732
  189.3 24.2 %all-to-all-start.3 = ((bf16[4,3,32,512]{3,2,1,0:T(8,128)(2,1)}), bf16[4,3,32,512]{3,2,1,0:T(8,128)(2,1)S(1)}, u32[]{:S(2)}, u32[]{:S(2)}) async-start(bf16[4,3,32,512]{3,2,1,0:T(8,128)(2,1)} %copy.26), calls=%async_computation.3 | async-start | bytes 786432 | tf_op jit(solution)/shard_map/all_to_all | solution.py:22

commit v2 on v1

v2 whole, which is shorter than its diff:
```python
import jax
import jax.numpy as jnp
from jax import lax
from jax.sharding import PartitionSpec as P

SIDE = 4


def far_groups(size):
    return [[near + SIDE * far for far in range(size // SIDE)] for near in range(SIDE)]


def exchanged(blocks, groups):
    return lax.all_to_all(blocks, "tok", 0, 0, axis_index_groups=groups, tiled=True)


def summed(blocks):
    return jnp.sum(blocks.astype(jnp.float32), axis=0)


def with_mate(block):
    size = lax.axis_size("tok")
    return lax.ppermute(block, "tok", [(i, i ^ 1) for i in range(size)])


def with_partner(block):
    size = lax.axis_size("tok")
    return lax.ppermute(block, "tok", [(i, i - i % SIDE + SIDE - 1 - i % SIDE) for i in range(size)])


def dotted(left, right, left_dim, right_dim):
    return lax.dot_general(
        left, right, (((left_dim,), (right_dim,)), ((), ())), preferred_element_type=jnp.float32
    )


def renormed(weights, gradient):
    old_values = weights.astype(jnp.float32)
    stepped = old_values - gradient
    old_norm = jnp.sqrt(jnp.sum(old_values * old_values, axis=-1, keepdims=True))
    new_norm = jnp.sqrt(jnp.sum(stepped * stepped, axis=-1, keepdims=True) + 1e-06)
    return (stepped * (old_norm / new_norm)).astype(jnp.bfloat16)


def split_rows(column):
    width = column.shape[-1]
    return tuple(column[:, part].reshape(-1, width) for part in range(3))


def output_piece(columns, queries):
    gate_rows, up_rows, down_rows = (
        jnp.concatenate(pieces) for pieces in zip(*(split_rows(column) for column in columns))
    )
    pre_gate = dotted(queries, gate_rows, 1, 1)
    pre_up = dotted(queries, up_rows, 1, 1)
    hidden = (jax.nn.silu(pre_gate) * pre_up).astype(jnp.bfloat16)
    return dotted(hidden, down_rows, 1, 0)


def partial_piece(column, key_rows, scaled):
    gate_rows, up_rows, down_rows = split_rows(column)
    pre_gate = dotted(key_rows, gate_rows, 1, 1)
    pre_up = dotted(key_rows, up_rows, 1, 1)
    hidden = (jax.nn.silu(pre_gate) * pre_up).astype(jnp.bfloat16)
    d_hidden = dotted(scaled, down_rows, 1, 1)
    sigmoid_gate = jax.nn.sigmoid(pre_gate)
    d_gate = (d_hidden * pre_up * sigmoid_gate * (1.0 + pre_gate * (1.0 - sigmoid_gate))).astype(
        jnp.bfloat16
    )
    d_up = (d_hidden * jax.nn.silu(pre_gate)).astype(jnp.bfloat16)
    block = column.shape[:1] + column.shape[2:]
    return jnp.stack(
        [
            dotted(left, right, 0, 0).reshape(block)
            for left, right in ((d_gate, key_rows), (d_up, key_rows), (hidden, scaled))
        ],
        axis=1,
    )


def tick_inputs(qkv, rates):
    queries, key_rows, value_rows = (qkv[:, i, :] for i in range(3))
    scaled = (-rates[:, None] * value_rows.astype(jnp.float32)).astype(jnp.bfloat16)
    pairs = jnp.stack([key_rows, scaled])
    mate_pairs = with_mate(pairs)
    mate_queries = with_mate(queries)
    key_rows, scaled = jnp.concatenate([pairs, mate_pairs], axis=1)
    return queries, mate_queries, key_rows, scaled


def finished(own_output, returned):
    return (own_output + returned.astype(jnp.float32)).astype(jnp.bfloat16)


def fast_tick(own_rows, inputs, pending=()):
    size = lax.axis_size("tok")
    own_queries, mate_queries, key_rows, scaled = inputs
    own_column = lax.all_gather(own_rows, "tok", axis=0, axis_index_groups=far_groups(size))
    partner_column = with_partner(own_column)
    own_column, *pending = lax.optimization_barrier((own_column, *pending))
    earlier = finished(*pending) if pending else None
    partner_column, earlier = lax.optimization_barrier((partner_column, earlier))
    own_partial = partial_piece(own_column, key_rows, scaled)
    partner_partial = partial_piece(partner_column, key_rows, scaled).astype(jnp.bfloat16)
    reduced = with_partner(partner_partial)
    column_sum = own_partial + reduced.astype(jnp.float32)
    scattered = exchanged(column_sum.astype(jnp.bfloat16), far_groups(size))
    gradient = summed(scattered)
    columns = (own_column, partner_column)
    mate_output = output_piece(columns, mate_queries).astype(jnp.bfloat16)
    returned = with_mate(mate_output)
    pending = (output_piece(columns, own_queries), returned)
    return pending, renormed(own_rows, gradient), earlier


def both_ticks(entering, fresh, qkv_first, qkv_second, rates_first, rates_second):
    groups = lax.axis_size("seq")
    own_rows = jnp.swapaxes(entering[0], 0, 1)
    fresh_rows = jnp.swapaxes(fresh, 0, 1)
    first_inputs = tick_inputs(qkv_first[0], rates_first[0])
    second_inputs = tick_inputs(qkv_second[0], rates_second[0])
    pending, new_rows, _ = fast_tick(own_rows, first_inputs)
    last_group = lax.axis_index("seq") == groups - 1
    handed = jnp.where(last_group, fresh_rows, new_rows)
    second_rows = lax.ppermute(handed, "seq", [(i, (i + 1) % groups) for i in range(groups)])
    last_pending, leaving_rows, out_first = fast_tick(second_rows, second_inputs, pending)
    out_second = finished(*last_pending)
    leaving = jnp.swapaxes(leaving_rows, 0, 1)
    return (out_first[None], out_second[None], leaving[None])


def solution(mesh):
    placed = (
        P("seq", "tok", None, None),
        P("tok", None, None),
        P("seq", "tok", None, None),
        P("seq", "tok", None, None),
        P("seq", "tok"),
        P("seq", "tok"),
    )
    return jax.shard_map(
        both_ticks,
        mesh=mesh,
        in_specs=placed,
        out_specs=(P("seq", "tok", None), P("seq", "tok", None), P("seq", "tok", None, None)),
        check_vma=False,
    )
```

time: 215 us -> 179 us (0.83)
  blocking collectives: 139 us -> 53.7 us
  starting transfers between devices: 15.5 us -> 46.6 us
  matrix products: 11.6 us -> 25.6 us
  other arithmetic: 2.39 us -> 7.32 us
    all_gather x6 -> x2, blocking collectives: 106 us -> 53.7 us  [fast_tick(): lax.all_gather(own_rows, 'tok', axis=0, axis_index_groups=far_groups(size))]
    all_to_all x2 -> x0, blocking collectives: 33.6 us -> none  [exchanged(): lax.all_to_all(blocks, 'tok', 0, 0, axis_index_groups=groups, tiled=True)]
    ppermute x1 -> x11, starting transfers between devices: 1.92 us -> 32.9 us  [the longest x6 17.1 us: with_mate(): return lax.ppermute(block, 'tok', [(i, i ^ 1) for i in range(size)])]
    all_to_all x2, waiting for transfers between devices: 33.6 us -> 4.79 us  [exchanged(): lax.all_to_all(blocks, 'tok', 0, 0, axis_index_groups=groups, tiled=True)]
    ppermute x1 -> x11, waiting for transfers between devices: 6.67 us -> 33.6 us  [the longest x4 19.1 us: with_partner(): lax.ppermute(block, 'tok', [(i, i - i % SIDE + SIDE - 1 - i % SIDE) for i...]
    dot_general x14 -> x32, matrix products: 11.6 us -> 25.6 us  [dotted(): lax.dot_general(left, right, (((left_dim,), (right_dim,)), ((), ())), pre...]
    convert_element_type x0 -> x5, other arithmetic: none -> 2.56 us  [the longest x1 1.99 us: finished(): return (own_output + returned.astype(jnp.float32)).astype(jnp.bfloat16)]
  transfers between devices with their start and end apart: 3 -> 13, of which waited for: 3 -> 7; matrix products, arithmetic and copies ran while one was open for 2% -> 19% of each run, Pallas kernels for 0% -> 0%
where the time goes in v2:
time: 179 us; the launch traced here: 178 us
  blocking collectives  53.7 us (30%)
  starting transfers between devices  46.6 us (26%)
  waiting for transfers between devices  38.4 us (21%)
  matrix products  25.6 us (14%)
  other arithmetic  7.32 us (4%)
  local copies, waits for them, and re-layouts  4.87 us (3%)
    all_gather x2, blocking collectives, fast_tick(): lax.all_gather(own_rows, 'tok', axis=0, axis_index_groups=far_groups(size))  53.7 us
    dot_general x32, matrix products, dotted(): lax.dot_general(left, right, (((left_dim,), (right_dim,)), ((), ())), pre...  25.6 us
    ppermute x4, waiting for transfers between devices, with_partner(): lax.ppermute(block, 'tok', [(i, i - i % SIDE + SIDE - 1 - i % SIDE) for i...  19.1 us
    ppermute x6, starting transfers between devices, with_mate(): return lax.ppermute(block, 'tok', [(i, i ^ 1) for i in range(size)])  17.1 us
    ppermute x4, starting transfers between devices, with_partner(): lax.ppermute(block, 'tok', [(i, i - i % SIDE + SIDE - 1 - i % SIDE) for i...  13.8 us
    all_to_all x2, starting transfers between devices, exchanged(): lax.all_to_all(blocks, 'tok', 0, 0, axis_index_groups=groups, tiled=True)  13.6 us
    ppermute x6, waiting for transfers between devices, with_mate(): return lax.ppermute(block, 'tok', [(i, i ^ 1) for i in range(size)])  13 us
    all_to_all x2, waiting for transfers between devices, exchanged(): lax.all_to_all(blocks, 'tok', 0, 0, axis_index_groups=groups, tiled=True)  4.79 us
  transfers between devices with their start and end apart: 13, of which 7 were waited for; matrix products, arithmetic and copies ran while one was open for 19% of the time, Pallas kernels for 0%

profile of v2, /device:TPU:8, one launch (start us, length us, event | category | flops | bytes accessed | tf_op | source)
XLA Modules:
  0.0 177.7 jit_solution(2183721510325279149)
XLA Ops:
  0.6 0.8 neg.68
  1.4 2.1 %slice_bitcast_fusion.3 = (bf16[512,512]{1,0:T(8,128)(2,1)}, bf16[1,512,512]{2,1,0:T(8,128)(2,1)S(1)}) fusion(bf16[512,3,512]{2,0,1:T(8,128)(2,1)} %bitcast.235), kind=kLoop, calls=%fused_computation.98 | loop fusion | bytes 2097152 | tf_op jit(solution)/shard_map/squeeze | solution.py:82
  3.8 3.5 %collective-permute-start = (bf16[2,512,512]{2,1,0:T(8,128)(2,1)S(1)}, bf16[2,512,512]{2,1,0:T(8,128)(2,1)S(1)}, u32[]{:S(2)}, u32[]{:S(2)}) collective-permute-start(bf16[2,512,512]{2,1,0:T(8,128)(2,1)S(1)} %pad_maximum_fusion.2), channel_id=1, source_target_pairs={{0,1},{1,0},{2,3},{3,2},{4,5},{5,4},{6,7},{7,6},{8,9},{9,8},{10,11... | collective-permute-start | bytes 3145736 | tf_op jit(solution)/shard_map/ppermute | solution.py:23
  7.3 30.0 %all-gather = bf16[12,32,512]{2,1,0:T(8,128)(2,1)S(1)} all-gather(bf16[3,32,512]{2,1,0:T(8,128)(2,1)S(1)} %bitcast.259), channel_id=2, replica_groups={{0,4,8,12},{1,5,9,13},{2,6,10,14},{3,7,11,15},{16,20,24,28},{17,21,25,2..., dimensions={0}, use_global_device_ids=true | all-gather | bytes 491520 | tf_op jit(solution)/shard_map/all_gather | solution.py:98
  37.3 4.0 %collective-permute-start.1 = (bf16[4,3,32,512]{3,2,1,0:T(8,128)(2,1)S(1)}, bf16[4,3,32,512]{3,2,1,0:T(8,128)(2,1)S(1)}, u32[]{:S(2)}, u32[]{:S(2)}) collective-permute-start(bf16[4,3,32,512]{3,2,1,0:T(8,128)(2,1)S(1)} %bitcast.245), channel_id=1, source_target_pairs={{0,3},{1,2},{2,1},{3,0},{4,7},{5,6},{6,5},{7,4},{8,11},{9,10},{10,... | collective-permute-start | bytes 1179656 | tf_op jit(solution)/shard_map/ppermute | solution.py:28
  41.3 2.5 %collective-permute-start.5 = (bf16[512,512]{1,0:T(8,128)(2,1)}, bf16[512,512]{1,0:T(8,128)(2,1)}, u32[]{:S(2)}, u32[]{:S(2)}) collective-permute-start(bf16[512,512]{1,0:T(8,128)(2,1)} %get-tuple-element.19), channel_id=1, source_target_pairs={{0,1},{1,0},{2,3},{3,2},{4,5},{5,4},{6,7},{7,6},{8,9},{9,8},{10,11... | collective-permute-start | bytes 1572872 | tf_op jit(solution)/shard_map/ppermute | solution.py:23
  43.8 0.9 slice_bitcast_fusion.1
  44.7 3.3 %collective-permute-start.7 = (bf16[512,512]{1,0:T(8,128)(2,1)}, bf16[512,512]{1,0:T(8,128)(2,1)}, u32[]{:S(2)}, u32[]{:S(2)}) collective-permute-start(bf16[512,512]{1,0:T(8,128)(2,1)} %get-tuple-element.18), channel_id=1, source_target_pairs={{0,1},{1,0},{2,3},{3,2},{4,5},{5,4},{6,7},{7,6},{8,9},{9,8},{10,11... | collective-permute-start | bytes 1572872 | tf_op jit(solution)/shard_map/ppermute | solution.py:23
  48.5 0.2 copy-done.6
  48.7 0.5 convolution_bitcast_fusion.13
  49.2 0.5 convolution_bitcast_fusion.12
  49.7 0.5 convolution_bitcast_fusion.10
  50.2 0.5 convolution_bitcast_fusion.9
  50.7 0.6 multiply_convert_fusion.10
  51.3 0.3 fusion.8
  51.6 0.3 fusion.7
  51.9 0.3 fusion.6
  52.3 3.7 %collective-permute-start.2 = (bf16[4,3,32,512]{3,2,0,1:T(8,128)(2,1)S(1)}, bf16[4,3,32,512]{3,2,0,1:T(8,128)(2,1)S(1)}, u32[]{:S(2)}, u32[]{:S(2)}) collective-permute-start(bf16[4,3,32,512]{3,2,0,1:T(8,128)(2,1)S(1)} %pad_maximum_fusion.4), channel_id=1, source_target_pairs={{0,3},{1,2},{2,1},{3,0},{4,7},{5,6},{6,5},{7,4},{8,11},{9,10},{10,... | collective-permute-start | bytes 1179656 | tf_op jit(solution)/shard_map/ppermute | solution.py:28
  56.0 0.6 multiply_convert_fusion.13
  56.6 0.3 convolution_bitcast_fusion.17
  56.9 0.3 convolution_bitcast_fusion.18
  57.2 0.3 convolution_bitcast_fusion.19
  57.5 5.6 %collective-permute-done.2 = bf16[4,3,32,512]{3,2,0,1:T(8,128)(2,1)S(1)} collective-permute-done((bf16[4,3,32,512]{3,2,0,1:T(8,128)(2,1)S(1)}, bf16[4,3,32,512]{3,2,0,1:T(8,128)(2,1)S(1)}, u32[]{:S(2)}, u32[]{:S(2)}) %collective-permute-start.2) | collective-permute-done | bytes 393248 | tf_op jit(solution)/shard_map/ppermute | solution.py:28
  63.3 0.8 copy.9
  64.1 6.6 %all-to-all-start = ((bf16[4,3,32,512]{3,2,1,0:T(8,128)(2,1)}), bf16[4,3,32,512]{3,2,1,0:T(8,128)(2,1)S(1)}, u32[]{:S(2)}, u32[]{:S(2)}) async-start(bf16[4,3,32,512]{3,2,1,0:T(8,128)(2,1)} %copy.9), calls=%async_computation | async-start | bytes 786432 | tf_op jit(solution)/shard_map/all_to_all | solution.py:14
  70.6 1.1 pad_maximum_fusion.3
  71.7 1.9 %collective-permute-start.9 = (bf16[2,512,512]{2,1,0:T(8,128)(2,1)}, bf16[2,512,512]{2,1,0:T(8,128)(2,1)}, u32[]{:S(2)}, u32[]{:S(2)}) collective-permute-start(bf16[2,512,512]{2,1,0:T(8,128)(2,1)} %pad_maximum_fusion.3), channel_id=1, source_target_pairs={{0,1},{1,0},{2,3},{3,2},{4,5},{5,4},{6,7},{7,6},{8,9},{9,8},{10,11... | collective-permute-start | bytes 3145736 | tf_op jit(solution)/shard_map/ppermute | solution.py:23
  73.6 2.0 %convolution_bitcast_fusion.7 = f32[512,256]{0,1:T(8,128)} fusion(bf16[128,512]{1,0:T(8,128)(2,1)} %bitcast.264, bf16[128,512]{1,0:T(8,128)(2,1)S(1)} %bitcast.261, bf16[512,3,512]{2,0,1:T(8,128)(2,1)S(1)} %bitcast.237), kind=kOutput, calls=%fused_computation.11 | convolution fusion | flops 134742016 | bytes 1310720 | tf_op jit(solution)/shard_map/dot_general | solution.py:32
  75.7 2.7 %fusion.4 = f32[512,512]{1,0:T(8,128)} fusion(f32[512,256]{0,1:T(8,128)} %convolution_bitcast_fusion.7, bf16[128,512]{1,0:T(8,128)(2,1)} %bitcast.277, bf16[128,512]{1,0:T(8,128)(2,1)} %bitcast.274, bf16[128,512]{1,0:T(8,128)(2,1)S(1)} %bitcast.251, bf16[128,512]{1,0:T(8,128)(2,1)S(1)} %bitcast.248, bf16[512,3,512]{2,0,1:T(8,128)(2,1)S(1)} %bitcast.238), kind=kOutput, calls=%fused_computation.22 | convolution fusion | flops 270270464 | bytes 2621440 | tf_op jit(solution)/shard_map/dot_general | solution.py:32
  78.4 1.4 convolution_bitcast_fusion.4
  79.8 2.7 %convolution_convert_fusion.1 = bf16[512,512]{1,0:T(8,128)(2,1)} fusion(f32[512,256]{0,1:T(8,128)S(1)} %convolution_bitcast_fusion.4, bf16[512,512]{1,0:T(8,128)(2,1)} %collective-permute-done.5, bf16[128,512]{1,0:T(8,128)(2,1)} %bitcast.278, bf16[128,512]{1,0:T(8,128)(2,1)} %bitcast.275, bf16[128,512]{1,0:T(8,128)(2,1)} %bitcast.265, ...), kind=kOutput, calls=%fused_computation.3 | convolution fusion | flops 270532608 | bytes 2097152 | tf_op jit(solution)/shard_map/dot_general | solution.py:32
  82.5 3.9 %collective-permute-start.6 = (bf16[512,512]{1,0:T(8,128)(2,1)}, bf16[512,512]{1,0:T(8,128)(2,1)}, u32[]{:S(2)}, u32[]{:S(2)}) collective-permute-start(bf16[512,512]{1,0:T(8,128)(2,1)} %convolution_convert_fusion.1), channel_id=1, source_target_pairs={{0,1},{1,0},{2,3},{3,2},{4,5},{5,4},{6,7},{7,6},{8,9},{9,8},{10,11... | collective-permute-start | bytes 1572872 | tf_op jit(solution)/shard_map/ppermute | solution.py:23
  86.4 4.8 %all-to-all-done = bf16[4,3,32,512]{3,2,1,0:T(8,128)(2,1)S(1)} async-done(((bf16[4,3,32,512]{3,2,1,0:T(8,128)(2,1)}), bf16[4,3,32,512]{3,2,1,0:T(8,128)(2,1)S(1)}, u32[]{:S(2)}, u32[]{:S(2)}) %all-to-all-start) | async-done | bytes 393248 | tf_op jit(solution)/shard_map/all_to_all | solution.py:14
  91.5 2.1 %collective-permute-start.3 = (bf16[3,32,512]{2,1,0:T(8,128)(2,1)S(1)}, bf16[3,32,512]{2,1,0:T(8,128)(2,1)S(1)}, u32[]{:S(2)}, u32[]{:S(2)}) collective-permute-start(bf16[3,32,512]{2,1,0:T(8,128)(2,1)S(1)} %fusion.91), channel_id=1, source_target_pairs={{0,16},{16,32},{32,48},{48,64},{64,80},{80,96},{96,112},{112,128},... | collective-permute-start | bytes 294920 | tf_op jit(solution)/shard_map/ppermute | solution.py:125
  93.6 3.9 %collective-permute-done.9 = bf16[2,512,512]{2,1,0:T(8,128)(2,1)} collective-permute-done((bf16[2,512,512]{2,1,0:T(8,128)(2,1)}, bf16[2,512,512]{2,1,0:T(8,128)(2,1)}, u32[]{:S(2)}, u32[]{:S(2)}) %collective-permute-start.9) | collective-permute-done | bytes 1048608 | tf_op jit(solution)/shard_map/ppermute | solution.py:23
  97.5 1.4 pad_maximum_fusion.1
  98.8 1.5 collective-permute-done.3
  100.3 23.7 %all-gather.1 = bf16[12,32,512]{2,1,0:T(8,128)(2,1)S(1)} all-gather(bf16[3,32,512]{2,1,0:T(8,128)(2,1)S(1)} %collective-permute-done.3), channel_id=3, replica_groups={{0,4,8,12},{1,5,9,13},{2,6,10,14},{3,7,11,15},{16,20,24,28},{17,21,25,2..., dimensions={0}, use_global_device_ids=true | all-gather | bytes 491520 | tf_op jit(solution)/shard_map/all_gather | solution.py:98
  124.0 3.0 %collective-permute-start.4 = (bf16[4,3,32,512]{3,2,1,0:T(8,128)(2,1)S(1)}, bf16[4,3,32,512]{3,2,1,0:T(8,128)(2,1)S(1)}, u32[]{:S(2)}, u32[]{:S(2)}) collective-permute-start(bf16[4,3,32,512]{3,2,1,0:T(8,128)(2,1)S(1)} %bitcast.243), channel_id=1, source_target_pairs={{0,3},{1,2},{2,1},{3,0},{4,7},{5,6},{6,5},{7,4},{8,11},{9,10},{10,... | collective-permute-start | bytes 1179656 | tf_op jit(solution)/shard_map/ppermute | solution.py:28
  127.1 2.0 %add_convert_fusion.1 = bf16[512,512]{1,0:T(8,128)(2,1)} fusion(f32[512,512]{1,0:T(8,128)S(1)} %copy-done.3, bf16[512,512]{1,0:T(8,128)(2,1)} %collective-permute-done.6), kind=kLoop, calls=%fused_computation.79 | loop fusion | flops 786432 | bytes 2097152 | tf_op jit(solution)/shard_map/convert_element_type | solution.py:92
  129.1 0.5 fusion.30
  129.6 0.5 fusion.26
  130.1 0.6 multiply_convert_fusion.5
  130.7 6.6 %collective-permute-done.4 = bf16[4,3,32,512]{3,2,1,0:T(8,128)(2,1)S(1)} collective-permute-done((bf16[4,3,32,512]{3,2,1,0:T(8,128)(2,1)S(1)}, bf16[4,3,32,512]{3,2,1,0:T(8,128)(2,1)S(1)}, u32[]{:S(2)}, u32[]{:S(2)}) %collective-permute-start.4) | collective-permute-done | bytes 393248 | tf_op jit(solution)/shard_map/ppermute | solution.py:28
  137.4 0.5 fusion.28
  137.8 0.5 fusion.22
  138.3 0.6 multiply_convert_fusion.2
  138.9 0.3 fusion.11
  139.3 0.3 fusion.10
  139.6 0.3 fusion.9
  140.0 3.1 %collective-permute-start.10 = (bf16[4,3,32,512]{3,2,0,1:T(8,128)(2,1)S(1)}, bf16[4,3,32,512]{3,2,0,1:T(8,128)(2,1)S(1)}, u32[]{:S(2)}, u32[]{:S(2)}) collective-permute-start(bf16[4,3,32,512]{3,2,0,1:T(8,128)(2,1)S(1)} %pad_maximum_fusion.5), channel_id=1, source_target_pairs={{0,3},{1,2},{2,1},{3,0},{4,7},{5,6},{6,5},{7,4},{8,11},{9,10},{10,... | collective-permute-start | bytes 1179656 | tf_op jit(solution)/shard_map/ppermute | solution.py:28
  143.1 0.3 convolution_bitcast_fusion.14
  143.4 0.3 convolution_bitcast_fusion.15
  143.7 0.3 convolution_bitcast_fusion.16
  144.0 6.8 %collective-permute-done.10 = bf16[4,3,32,512]{3,2,0,1:T(8,128)(2,1)S(1)} collective-permute-done((bf16[4,3,32,512]{3,2,0,1:T(8,128)(2,1)S(1)}, bf16[4,3,32,512]{3,2,0,1:T(8,128)(2,1)S(1)}, u32[]{:S(2)}, u32[]{:S(2)}) %collective-permute-start.10) | collective-permute-done | bytes 393248 | tf_op jit(solution)/shard_map/ppermute | solution.py:28
  151.0 0.8 copy.10
  151.7 7.1 %all-to-all-start.1 = ((bf16[4,3,32,512]{3,2,1,0:T(8,128)(2,1)}), bf16[4,3,32,512]{3,2,1,0:T(8,128)(2,1)S(1)}, u32[]{:S(2)}, u32[]{:S(2)}) async-start(bf16[4,3,32,512]{3,2,1,0:T(8,128)(2,1)} %copy.10), calls=%async_computation.1 | async-start | bytes 786432 | tf_op jit(solution)/shard_map/all_to_all | solution.py:14
  158.8 1.4 convolution_bitcast_fusion
  160.2 2.7 %convolution_convert_fusion = bf16[512,512]{1,0:T(8,128)(2,1)} fusion(f32[512,256]{0,1:T(8,128)S(1)} %convolution_bitcast_fusion, bf16[512,512]{1,0:T(8,128)(2,1)} %collective-permute-done.7, bf16[128,512]{1,0:T(8,128)(2,1)S(1)} %bitcast.283, bf16[128,512]{1,0:T(8,128)(2,1)S(1)} %bitcast.280, bf16[128,512]{1,0:T(8,128)(2,1)S(1)} %bitcast.270, ...), kind=kOutput, calls=%fused_computation.2 | convolution fusion | flops 270532608 | bytes 2097152 | tf_op jit(solution)/shard_map/dot_general | solution.py:32
  162.9 1.9 %collective-permute-start.8 = (bf16[512,512]{1,0:T(8,128)(2,1)}, bf16[512,512]{1,0:T(8,128)(2,1)}, u32[]{:S(2)}, u32[]{:S(2)}) collective-permute-start(bf16[512,512]{1,0:T(8,128)(2,1)} %convolution_convert_fusion), channel_id=1, source_target_pairs={{0,1},{1,0},{2,3},{3,2},{4,5},{5,4},{6,7},{7,6},{8,9},{9,8},{10,11... | collective-permute-start | bytes 1572872 | tf_op jit(solution)/shard_map/ppermute | solution.py:23
  164.8 0.3 convolution_bitcast_fusion.3
  165.1 9.1 %collective-permute-done.8 = bf16[512,512]{1,0:T(8,128)(2,1)} collective-permute-done((bf16[512,512]{1,0:T(8,128)(2,1)}, bf16[512,512]{1,0:T(8,128)(2,1)}, u32[]{:S(2)}, u32[]{:S(2)}) %collective-permute-start.8) | collective-permute-done | bytes 524320 | tf_op jit(solution)/shard_map/ppermute | solution.py:23
  174.3 2.5 %fusion.54 = bf16[1,512,512]{2,1,0:T(8,128)(2,1)} fusion(bf16[512,512]{1,0:T(8,128)(2,1)} %collective-permute-done.8, f32[512,256]{0,1:T(8,128)S(1)} %convolution_bitcast_fusion.3, bf16[128,512]{1,0:T(8,128)(2,1)S(1)} %bitcast.284, bf16[128,512]{1,0:T(8,128)(2,1)S(1)} %bitcast.281, bf16[128,512]{1,0:T(8,128)(2,1)S(1)} %bitcast.258, ...), kind=kOutput, calls=%fused_computation.94 | convolution fusion | flops 271056896 | bytes 2621440 | tf_op jit(solution)/shard_map/dot_general | solution.py:32
  176.9 0.7 fusion.92
  (45 shorter events, 1.5 us)
Async XLA Ops:
  0.6 2.9 %copy-start = (bf16[1,512,3,512]{3,1,2,0:T(8,128)(2,1)S(1)}, bf16[1,512,3,512]{3,1,2,0:T(8,128)(2,1)}, u32[]{:S(2)}) copy-start(bf16[1,512,3,512]{3,1,2,0:T(8,128)(2,1)} %param.8) | copy-start | bytes 4718596
  3.5 3.8 %copy-start.4 = (bf16[1,32,3,512]{3,1,2,0:T(8,128)(2,1)S(1)}, bf16[1,32,3,512]{3,1,2,0:T(8,128)(2,1)}, u32[]{:S(2)}) copy-start(bf16[1,32,3,512]{3,1,2,0:T(8,128)(2,1)} %param.6) | copy-start | bytes 294916
  3.5 40.3 %copy-start.1 = (bf16[1,512,3,512]{3,1,2,0:T(8,128)(2,1)S(1)}, bf16[1,512,3,512]{3,1,2,0:T(8,128)(2,1)}, u32[]{:S(2)}) copy-start(bf16[1,512,3,512]{3,1,2,0:T(8,128)(2,1)} %param.9) | copy-start | bytes 4718596
  3.7 44.4 %copy-start.9 = (f32[1,512]{1,0:T(1,128)S(1)}, f32[1,512]{1,0:T(1,128)}, u32[]{:S(2)}) copy-start(f32[1,512]{1,0:T(1,128)} %param.11) | copy-start | bytes 6148
  3.8 44.5 %collective-permute-start = (bf16[2,512,512]{2,1,0:T(8,128)(2,1)S(1)}, bf16[2,512,512]{2,1,0:T(8,128)(2,1)S(1)}, u32[]{:S(2)}, u32[]{:S(2)}) collective-permute-start(bf16[2,512,512]{2,1,0:T(8,128)(2,1)S(1)} %pad_maximum_fusion.2), channel_id=1, source_target_pairs={{0,1},{1,0},{2,3},{3,2},{4,5},{5,4},{6,7},{7,6},{8,9},{9,8},{10,11... | collective-permute-start | bytes 3145736 | tf_op jit(solution)/shard_map/ppermute | solution.py:23
  37.3 11.0 %collective-permute-start.1 = (bf16[4,3,32,512]{3,2,1,0:T(8,128)(2,1)S(1)}, bf16[4,3,32,512]{3,2,1,0:T(8,128)(2,1)S(1)}, u32[]{:S(2)}, u32[]{:S(2)}) collective-permute-start(bf16[4,3,32,512]{3,2,1,0:T(8,128)(2,1)S(1)} %bitcast.245), channel_id=1, source_target_pairs={{0,3},{1,2},{2,1},{3,0},{4,7},{5,6},{6,5},{7,4},{8,11},{9,10},{10,... | collective-permute-start | bytes 1179656 | tf_op jit(solution)/shard_map/ppermute | solution.py:28
  41.3 37.1 %collective-permute-start.5 = (bf16[512,512]{1,0:T(8,128)(2,1)}, bf16[512,512]{1,0:T(8,128)(2,1)}, u32[]{:S(2)}, u32[]{:S(2)}) collective-permute-start(bf16[512,512]{1,0:T(8,128)(2,1)} %get-tuple-element.19), channel_id=1, source_target_pairs={{0,1},{1,0},{2,3},{3,2},{4,5},{5,4},{6,7},{7,6},{8,9},{9,8},{10,11... | collective-permute-start | bytes 1572872 | tf_op jit(solution)/shard_map/ppermute | solution.py:23
  44.7 114.1 %collective-permute-start.7 = (bf16[512,512]{1,0:T(8,128)(2,1)}, bf16[512,512]{1,0:T(8,128)(2,1)}, u32[]{:S(2)}, u32[]{:S(2)}) collective-permute-start(bf16[512,512]{1,0:T(8,128)(2,1)} %get-tuple-element.18), channel_id=1, source_target_pairs={{0,1},{1,0},{2,3},{3,2},{4,5},{5,4},{6,7},{7,6},{8,9},{9,8},{10,11... | collective-permute-start | bytes 1572872 | tf_op jit(solution)/shard_map/ppermute | solution.py:23
  48.1 0.7 copy-start.6
  48.3 1.4 copy-start.7
  48.3 2.3 %copy-start.5 = (bf16[4,1,32,512]{3,2,1,0:T(8,128)(2,1)}, bf16[4,1,32,512]{3,2,1,0:T(8,128)(2,1)S(1)}, u32[]{:S(2)}) copy-start(bf16[4,1,32,512]{3,2,1,0:T(8,128)(2,1)S(1)} %get-tuple-element.40) | copy-start | bytes 393220
  52.3 10.9 %collective-permute-start.2 = (bf16[4,3,32,512]{3,2,0,1:T(8,128)(2,1)S(1)}, bf16[4,3,32,512]{3,2,0,1:T(8,128)(2,1)S(1)}, u32[]{:S(2)}, u32[]{:S(2)}) collective-permute-start(bf16[4,3,32,512]{3,2,0,1:T(8,128)(2,1)S(1)} %pad_maximum_fusion.4), channel_id=1, source_target_pairs={{0,3},{1,2},{2,1},{3,0},{4,7},{5,6},{6,5},{7,4},{8,11},{9,10},{10,... | collective-permute-start | bytes 1179656 | tf_op jit(solution)/shard_map/ppermute | solution.py:28
  64.1 27.1 %all-to-all-start = ((bf16[4,3,32,512]{3,2,1,0:T(8,128)(2,1)}), bf16[4,3,32,512]{3,2,1,0:T(8,128)(2,1)S(1)}, u32[]{:S(2)}, u32[]{:S(2)}) async-start(bf16[4,3,32,512]{3,2,1,0:T(8,128)(2,1)} %copy.9), calls=%async_computation | async-start | bytes 786432 | tf_op jit(solution)/shard_map/all_to_all | solution.py:14
  71.7 25.7 %collective-permute-start.9 = (bf16[2,512,512]{2,1,0:T(8,128)(2,1)}, bf16[2,512,512]{2,1,0:T(8,128)(2,1)}, u32[]{:S(2)}, u32[]{:S(2)}) collective-permute-start(bf16[2,512,512]{2,1,0:T(8,128)(2,1)} %pad_maximum_fusion.3), channel_id=1, source_target_pairs={{0,1},{1,0},{2,3},{3,2},{4,5},{5,4},{6,7},{7,6},{8,9},{9,8},{10,11... | collective-permute-start | bytes 3145736 | tf_op jit(solution)/shard_map/ppermute | solution.py:23
  79.8 11.6 %copy-start.8 = (bf16[32,3,512]{2,0,1:T(8,128)(2,1)S(1)}, bf16[32,3,512]{2,0,1:T(8,128)(2,1)}, u32[]{:S(2)}) copy-start(bf16[32,3,512]{2,0,1:T(8,128)(2,1)} %param.7) | copy-start | bytes 294916
  82.5 44.6 %collective-permute-start.6 = (bf16[512,512]{1,0:T(8,128)(2,1)}, bf16[512,512]{1,0:T(8,128)(2,1)}, u32[]{:S(2)}, u32[]{:S(2)}) collective-permute-start(bf16[512,512]{1,0:T(8,128)(2,1)} %convolution_convert_fusion.1), channel_id=1, source_target_pairs={{0,1},{1,0},{2,3},{3,2},{4,5},{5,4},{6,7},{7,6},{8,9},{9,8},{10,11... | collective-permute-start | bytes 1572872 | tf_op jit(solution)/shard_map/ppermute | solution.py:23
  91.5 35.6 %copy-start.3 = (f32[512,512]{1,0:T(8,128)S(1)}, f32[512,512]{1,0:T(8,128)}, u32[]{:S(2)}) copy-start(f32[512,512]{1,0:T(8,128)} %fusion.4) | copy-start | bytes 3145732
  91.5 8.8 %collective-permute-start.3 = (bf16[3,32,512]{2,1,0:T(8,128)(2,1)S(1)}, bf16[3,32,512]{2,1,0:T(8,128)(2,1)S(1)}, u32[]{:S(2)}, u32[]{:S(2)}) collective-permute-start(bf16[3,32,512]{2,1,0:T(8,128)(2,1)S(1)} %fusion.91), channel_id=1, source_target_pairs={{0,16},{16,32},{32,48},{48,64},{64,80},{80,96},{96,112},{112,128},... | collective-permute-start | bytes 294920 | tf_op jit(solution)/shard_map/ppermute | solution.py:125
  124.0 13.3 %collective-permute-start.4 = (bf16[4,3,32,512]{3,2,1,0:T(8,128)(2,1)S(1)}, bf16[4,3,32,512]{3,2,1,0:T(8,128)(2,1)S(1)}, u32[]{:S(2)}, u32[]{:S(2)}) collective-permute-start(bf16[4,3,32,512]{3,2,1,0:T(8,128)(2,1)S(1)} %bitcast.243), channel_id=1, source_target_pairs={{0,3},{1,2},{2,1},{3,0},{4,7},{5,6},{6,5},{7,4},{8,11},{9,10},{10,... | collective-permute-start | bytes 1179656 | tf_op jit(solution)/shard_map/ppermute | solution.py:28
  140.0 10.9 %collective-permute-start.10 = (bf16[4,3,32,512]{3,2,0,1:T(8,128)(2,1)S(1)}, bf16[4,3,32,512]{3,2,0,1:T(8,128)(2,1)S(1)}, u32[]{:S(2)}, u32[]{:S(2)}) collective-permute-start(bf16[4,3,32,512]{3,2,0,1:T(8,128)(2,1)S(1)} %pad_maximum_fusion.5), channel_id=1, source_target_pairs={{0,3},{1,2},{2,1},{3,0},{4,7},{5,6},{6,5},{7,4},{8,11},{9,10},{10,... | collective-permute-start | bytes 1179656 | tf_op jit(solution)/shard_map/ppermute | solution.py:28
  151.7 25.0 %all-to-all-start.1 = ((bf16[4,3,32,512]{3,2,1,0:T(8,128)(2,1)}), bf16[4,3,32,512]{3,2,1,0:T(8,128)(2,1)S(1)}, u32[]{:S(2)}, u32[]{:S(2)}) async-start(bf16[4,3,32,512]{3,2,1,0:T(8,128)(2,1)} %copy.10), calls=%async_computation.1 | async-start | bytes 786432 | tf_op jit(solution)/shard_map/all_to_all | solution.py:14
  160.2 4.6 %copy-start.2 = (bf16[1,512,3,512]{3,1,2,0:T(8,128)(2,1)S(1)}, bf16[1,512,3,512]{3,1,2,0:T(8,128)(2,1)}, u32[]{:S(2)}) copy-start(bf16[1,512,3,512]{3,1,2,0:T(8,128)(2,1)} %param.9) | copy-start | bytes 4718596
  162.9 11.4 %collective-permute-start.8 = (bf16[512,512]{1,0:T(8,128)(2,1)}, bf16[512,512]{1,0:T(8,128)(2,1)}, u32[]{:S(2)}, u32[]{:S(2)}) collective-permute-start(bf16[512,512]{1,0:T(8,128)(2,1)} %convolution_convert_fusion), channel_id=1, source_target_pairs={{0,1},{1,0},{2,3},{3,2},{4,5},{5,4},{6,7},{7,6},{8,9},{9,8},{10,11... | collective-permute-start | bytes 1572872 | tf_op jit(solution)/shard_map/ppermute | solution.py:23
